TPU v7x, 256 devices: a whole 4x4x8 slice. The times are simulated.
256 devices in a mesh: tp: 8 (over x, z_hi), cp: 32 (over z_lo, y, core).
Axes of the slice: x: 4, y: 4, z: 8 (z_hi: 2, z_lo: 4; z = z_hi * 4 + z_lo), core: 2. Of those that a mesh axis runs over, the one named last changes fastest.
Arguments:
- signal: bfloat16 [4096, 4096], P('cp', 'tp'), may hold values from -6 to 6
- cotangent: bfloat16 [4096, 4096], P('cp', 'tp'), may hold values from -0.09375 to 0.09375
- long_filter: bfloat16 [4096, 512], P('cp'), may hold values from -6 to 6
Outputs:
- grad_signal: bfloat16 [4096, 4096], P('cp', 'tp')
- grad_filter: bfloat16 [4096, 512], P('cp')
All inputs are finite; a program needn't handle non-finite values.
Results may differ from a plain program's by a relative error of at most 0.0015.
Values may be sent and summed in bfloat16 or wider, within the bound.
A program may use at most 64 MiB of HBM per device.

v0:
```python
import functools

import jax
import jax.numpy as jnp
import ml_dtypes
import numpy as np
from jax import lax
from jax.experimental import pallas as pl
from jax.experimental.pallas import tpu as pltpu
from jax.sharding import PartitionSpec as P

MESH = pl.DeviceIdType.MESH
bf16, f32 = jnp.bfloat16, jnp.float32
LANES = 128


def split_np(table):
    high = table.astype(ml_dtypes.bfloat16)
    low = (table - high.astype(np.float64)).astype(ml_dtypes.bfloat16)
    return high, low


def make_tables(blocks):
    half = 2 * blocks
    total = half * LANES
    w = np.arange(blocks) + 0.5
    k = np.arange(blocks)
    angle = 2 * np.pi * np.outer(w, k) / half
    pair = np.eye(2)
    cos_wk, sin_wk = np.kron(np.cos(angle), pair), np.kron(np.sin(angle), pair)
    filt = np.concatenate([cos_wk, -sin_wk], axis=0)
    both = np.zeros((2, 2, blocks, 2, blocks, 2, 2))
    for a in range(2):
        for c in range(2):
            both[a, 0, :, c, :, a, c] = np.cos(angle)
            both[a, 1, :, c, :, a, c] = -np.sin(angle)
    both = both.reshape(8 * blocks, 4 * blocks)
    lane = np.arange(LANES)
    twist = 2 * np.pi * np.outer(np.repeat(w, 2), lane) / total
    turn = 2 * np.pi * np.outer(lane, lane) / LANES
    cos_t, sin_t = np.cos(turn), np.sin(turn)
    forward = np.block([[cos_t, -sin_t], [sin_t, cos_t]])
    back = np.concatenate([cos_wk.T, -sin_wk.T], axis=1) * (2.0 / total)
    both_h, both_l = split_np(both)
    filt_h, filt_l = split_np(filt)
    forw_h, forw_l = split_np(forward)
    inv_h, inv_l = split_np(forward.T)
    back_h, back_l = split_np(back)
    tables = (
        np.concatenate([both_h, both_l], axis=1),
        np.concatenate([filt_h, filt_l], axis=1),
        np.stack([np.cos(twist), np.sin(twist)]).astype(np.float32),
        np.stack([forw_h, forw_l]),
        np.stack([inv_h, inv_l]),
        np.concatenate([back_h, back_h, back_l], axis=1),
    )
    return tables


def permutation(groups):
    table = np.zeros((groups, 2, 2, 2, groups, 2), np.float32)
    for d in range(groups):
        for a in range(2):
            for c in range(2):
                table[d, a, c, a, d, c] = 1
    return table.reshape(4 * groups, 4 * groups)


def dot(left, right):
    return lax.dot_general(left, right, (((1,), (0,)), ((), ())), preferred_element_type=f32)


def dot_nt(left, right):
    return lax.dot_general(left, right, (((1,), (1,)), ((), ())), preferred_element_type=f32)


def split(value):
    high = value.astype(bf16)
    low = (value - high.astype(f32)).astype(bf16)
    return high, low


def dot3(value, table_ref):
    high, low = split(value)
    top, bottom = table_ref[0], table_ref[1]
    return dot(high, top) + (dot(low, top) + dot(high, bottom))


def exchange(
    groups,
    blocks,
    sig_hbm,
    cot_hbm,
    fil_hbm,
    *refs,
):
    tables_hbm, rest = refs[:7], refs[7:]
    out_ref = rest[0]
    sig, cot, fil = rest[1:4]
    both, filt, twist, forw, inv, back, perm = rest[4:11]
    (send, send_f, recv, recv_f, ready, back_in) = rest[11:17]
    (load_sem, send_sem, recv_sem, send_f_sem, recv_f_sem, out_sem, in_sem, exit_sem) = rest[17:]
    t = lax.axis_index("tp")
    p = lax.axis_index("cp")
    me = t * blocks + p
    devices = groups * blocks

    def peers(act):
        def group_step(a, _):
            group = lax.rem(t + a, groups)

            def place_step(b, _):
                place = lax.rem(p + b, blocks)
                act(group, place)
                return 0

            lax.fori_loop(jnp.where(a == 0, 1, 0), blocks, place_step, 0)
            return 0

        lax.fori_loop(0, groups, group_step, 0)

    loads = [
        pltpu.make_async_copy(source, target, load_sem.at[i])
        for i, (source, target) in enumerate(
            zip(
                (sig_hbm, cot_hbm, fil_hbm) + tuple(tables_hbm),
                (sig, cot, fil, both, filt, twist, forw, inv, back, perm),
                strict=True,
            )
        )
    ]
    for load in loads:
        load.start()

    barrier = pltpu.get_barrier_semaphore()

    def greet(group, place):
        pl.semaphore_signal(barrier, inc=1, device_id=(group, place), device_id_type=MESH)

    peers(greet)
    for load in loads:
        load.wait()

    rows = perm[...]
    eye = (
        lax.broadcasted_iota(jnp.int32, (LANES, LANES), 0)
        == lax.broadcasted_iota(jnp.int32, (LANES, LANES), 1)
    ).astype(f32).astype(bf16)
    quarters = 2 * devices // LANES
    per = LANES // 2
    for q in range(quarters):
        cols = pl.ds(q * LANES, LANES)
        pair = jnp.concatenate([sig[:, cols], cot[:, cols]], axis=1)
        moved = dot_nt(rows, pair)
        send[pl.ds(q * per, per)] = moved.reshape(per, 4, LANES).astype(bf16)
        moved = dot_nt(eye, fil[:, cols])
        send_f[pl.ds(q * per, per)] = moved.reshape(per, 2, LANES).astype(bf16)

    pl.semaphore_wait(barrier, devices - 1)

    pltpu.make_async_copy(send_f.at[me], recv_f.at[p], recv_f_sem).start()

    def filter_step(b, _):
        place = lax.rem(p + b, blocks)
        pltpu.make_async_remote_copy(
            send_f.at[t * blocks + place],
            recv_f.at[p],
            send_f_sem,
            recv_f_sem,
            device_id=(t, place),
            device_id_type=MESH,
        ).start()
        return 0

    lax.fori_loop(1, blocks, filter_step, 0)
    pltpu.make_async_copy(send.at[me], recv.at[me], recv_sem).start()

    def give(group, place):
        pltpu.make_async_remote_copy(
            send.at[group * blocks + place],
            recv.at[me],
            send_sem,
            recv_sem,
            device_id=(group, place),
            device_id_type=MESH,
        ).start()

    peers(give)

    turn_c, turn_s = twist[0], twist[1]
    width = 2 * blocks

    def spectrum(real, imag):
        turned = jnp.concatenate(
            [real * turn_c + imag * turn_s, imag * turn_c - real * turn_s], axis=1
        )
        return dot3(turned, forw)

    pltpu.make_async_copy(recv_f, recv_f, recv_f_sem).wait()
    data = recv_f[...].reshape(2 * blocks, LANES)
    halves = dot(filt[...], jnp.concatenate([data, data], axis=0))
    h_spec = spectrum(halves[:width], halves[width:])
    h_real, h_imag = h_spec[:, :LANES], h_spec[:, LANES:]

    pltpu.make_async_copy(recv, recv, recv_sem).wait()
    sum_real = jnp.zeros((width, LANES), f32)
    sum_imag = jnp.zeros((width, LANES), f32)

    def inverse(real, imag):
        part = dot3(jnp.concatenate([real, imag], axis=1), inv)
        g_real, g_imag = part[:, :LANES], part[:, LANES:]
        turned = jnp.concatenate(
            [g_real * turn_c - g_imag * turn_s, g_real * turn_s + g_imag * turn_c], axis=0
        )
        high, low = split(turned)
        return dot(back[...], jnp.concatenate([high, low, high], axis=0))

    results = []
    for g in range(groups):
        data = recv[pl.ds(g * blocks, blocks)].reshape(4 * blocks, LANES)
        halves = dot(both[...], jnp.concatenate([data, data], axis=0))
        u_spec = spectrum(halves[:width], halves[width : 2 * width])
        d_spec = spectrum(halves[2 * width : 3 * width], halves[3 * width :])
        u_real, u_imag = u_spec[:, :LANES], u_spec[:, LANES:]
        d_real, d_imag = d_spec[:, :LANES], d_spec[:, LANES:]
        sum_real = sum_real + (u_real * d_real + u_imag * d_imag)
        sum_imag = sum_imag + (u_real * d_imag - u_imag * d_real)
        results.append(
            inverse(h_real * d_real + h_imag * d_imag, h_real * d_imag - h_imag * d_real)
        )
    gf = inverse(sum_real, sum_imag).reshape(blocks, 2, LANES)
    for g in range(groups):
        gs = results[g].reshape(blocks, 2, LANES)
        ready[pl.ds(g * blocks, blocks)] = jnp.concatenate([gs, gf], axis=1).astype(bf16)

    pltpu.make_async_copy(ready.at[me], back_in.at[me], in_sem).start()

    def give_back(group, place):
        pltpu.make_async_remote_copy(
            ready.at[group * blocks + place],
            back_in.at[me],
            out_sem,
            in_sem,
            device_id=(group, place),
            device_id_type=MESH,
        ).start()

    peers(give_back)
    pltpu.make_async_copy(back_in, back_in, in_sem).wait()
    done = pltpu.make_async_copy(back_in, out_ref, exit_sem)
    done.start()
    some = pl.ds(0, devices - 1)
    pltpu.make_async_copy(send.at[some], send.at[some], send_sem).wait()
    pltpu.make_async_copy(ready.at[some], ready.at[some], out_sem).wait()
    some = pl.ds(0, blocks - 1)
    pltpu.make_async_copy(send_f.at[some], send_f.at[some], send_f_sem).wait()
    done.wait()


def place_columns(quarters, in_ref, perm_ref, gs_ref, gf_ref):
    eye = (
        lax.broadcasted_iota(jnp.int32, (LANES, LANES), 0)
        == lax.broadcasted_iota(jnp.int32, (LANES, LANES), 1)
    ).astype(f32).astype(bf16)
    per = LANES // 2
    for q in range(quarters):
        block = in_ref[pl.ds(q * per, per)].reshape(4 * per, LANES)
        moved = dot_nt(eye, dot(perm_ref[...], block).astype(bf16)).astype(bf16)
        gs_ref[:, pl.ds(q * LANES, LANES)] = moved[:, :LANES]
        gf_ref[:, pl.ds(q * LANES, LANES)] = moved[:, LANES:]


def body(groups, blocks, signal, cotangent, long_filter):
    positions, columns = signal.shape
    devices = groups * blocks
    tables = make_tables(blocks)
    perm = permutation(LANES // 2)
    tables = tables + (perm.astype(ml_dtypes.bfloat16),)
    vmem = pltpu.VMEM
    dma = pltpu.SemaphoreType.DMA
    anywhere = pl.BlockSpec(memory_space=pl.ANY)
    width = 2 * blocks
    moved = pl.pallas_call(
        functools.partial(exchange, groups, blocks),
        name="exchange",
        out_shape=jax.ShapeDtypeStruct((devices, 4, LANES), bf16),
        in_specs=[anywhere] * (3 + len(tables)),
        out_specs=anywhere,
        scratch_shapes=[vmem((positions, columns), bf16)] * 3
        + [vmem(table.shape, table.dtype) for table in tables]
        + [
            vmem((devices, 4, LANES), bf16),
            vmem((devices, 2, LANES), bf16),
            vmem((devices, 4, LANES), bf16),
            vmem((blocks, 2, LANES), bf16),
            vmem((devices, 4, LANES), bf16),
            vmem((devices, 4, LANES), bf16),
            dma((3 + len(tables),)),
            dma(()),
            dma(()),
            dma(()),
            dma(()),
            dma(()),
            dma(()),
            dma(()),
        ],
        compiler_params=pltpu.CompilerParams(collective_id=0, has_side_effects=True),
    )(signal, cotangent, long_filter, *[jnp.asarray(table) for table in tables])
    whole = pl.BlockSpec(memory_space=pltpu.VMEM)
    return pl.pallas_call(
        functools.partial(place_columns, columns // LANES),
        name="place_columns",
        out_shape=(
            jax.ShapeDtypeStruct((positions, columns), bf16),
            jax.ShapeDtypeStruct((positions, columns), bf16),
        ),
        in_specs=[whole] * 2,
        out_specs=(whole, whole),
    )(moved, jnp.asarray(np.ascontiguousarray(perm.T).astype(ml_dtypes.bfloat16)))


def solution(mesh):
    in_specs = (P("cp", "tp"), P("cp", "tp"), P("cp", None))
    out_specs = (P("cp", "tp"), P("cp", None))
    run = functools.partial(body, mesh.shape["tp"], mesh.shape["cp"])
    return jax.shard_map(run, mesh=mesh, in_specs=in_specs, out_specs=out_specs, check_vma=False)
```

profile of v0, /device:TPU:1, one launch (start us, length us, event | category | flops | bytes accessed | tf_op | source)
XLA Modules:
  0.0 47.4 jit_solution(12089883783770295974)
XLA Ops:
  0.6 44.1 %exchange.1.in_ref = bf16[256,4,128]{2,1,0:T(4,128)(2,1)} custom-call(bf16[128,512]{1,0:T(8,128)(2,1)} %sig_hbm.1, bf16[128,512]{1,0:T(8,128)(2,1)} %cot_hbm.1, bf16[128,512]{1,0:T(8,128)(2,1)} %fil_hbm.1, bf16[256,256]{1,0:T(8,128)(2,1)} %constant.16.clone.refs_0_, bf16[128,128]{1,0:T(8,128)(2,1)} %constant.17.clone.refs_1_, ...), custom_call_target="tpu_custom_call" | custom-call | tf_op jit(solution)/shard_map/exchange/pallas_call | solution.py:283
  44.8 2.7 %place_columns.1 = (bf16[128,512]{1,0:T(8,128)(2,1)}, bf16[128,512]{1,0:T(8,128)(2,1)}) custom-call(bf16[256,4,128]{2,1,0:T(4,128)(2,1)} %exchange.1.in_ref, bf16[256,256]{1,0:T(8,128)(2,1)} %constant.23.clone.perm_ref), custom_call_target="tpu_custom_call" | custom-call | tf_op jit(solution)/shard_map/place_columns/pallas_call | solution.py:310
where the time goes:
time: 47.5 us; the launch traced here: 47.4 us
  Pallas kernels  46.8 us (99%)
  between operations  0.64 us (1%)
    pallas_call x1, Pallas kernels, body(): pl.pallas_call(functools.partial(exchange, groups, blocks), name='exchang...  44.1 us
    pallas_call x1, Pallas kernels, body(): pl.pallas_call(functools.partial(place_columns, columns // LANES), name='...  2.7 us

commit v1 on v0

v1 whole, which is shorter than its diff:
```python
import functools

import jax
import jax.numpy as jnp
import ml_dtypes
import numpy as np
from jax import lax
from jax.experimental import pallas as pl
from jax.experimental.pallas import tpu as pltpu
from jax.sharding import PartitionSpec as P

MESH = pl.DeviceIdType.MESH
bf16, f32 = jnp.bfloat16, jnp.float32
LANES = 128


def split_np(table):
    high = table.astype(ml_dtypes.bfloat16)
    low = (table - high.astype(np.float64)).astype(ml_dtypes.bfloat16)
    return high, low


def make_tables(blocks):
    half = 2 * blocks
    total = half * LANES
    w = np.arange(blocks) + 0.5
    k = np.arange(blocks)
    angle = 2 * np.pi * np.outer(w, k) / half
    pair = np.eye(2)
    cos_wk, sin_wk = np.kron(np.cos(angle), pair), np.kron(np.sin(angle), pair)
    filt = np.concatenate([cos_wk, -sin_wk], axis=0)
    both = np.zeros((2, 2, blocks, 2, blocks, 2, 2))
    for a in range(2):
        for c in range(2):
            both[a, 0, :, c, :, a, c] = np.cos(angle)
            both[a, 1, :, c, :, a, c] = -np.sin(angle)
    both = both.reshape(8 * blocks, 4 * blocks)
    lane = np.arange(LANES)
    twist = 2 * np.pi * np.outer(np.repeat(w, 2), lane) / total
    turn = 2 * np.pi * np.outer(lane, lane) / LANES
    cos_t, sin_t = np.cos(turn), np.sin(turn)
    forward = np.block([[cos_t, -sin_t], [sin_t, cos_t]])
    back = np.concatenate([cos_wk.T, -sin_wk.T], axis=1) * (2.0 / total)
    both_h, both_l = split_np(both)
    filt_h, filt_l = split_np(filt)
    forw_h, forw_l = split_np(forward)
    inv_h, inv_l = split_np(forward.T)
    back_h, back_l = split_np(back)
    tables = (
        np.concatenate([both_h, both_l], axis=1),
        np.concatenate([filt_h, filt_l], axis=1),
        np.stack([np.cos(twist), np.sin(twist)]).astype(np.float32),
        np.stack([forw_h, forw_l]),
        np.stack([inv_h, inv_l]),
        np.concatenate([back_h, back_h, back_l], axis=1),
    )
    return tables


def permutation(groups):
    table = np.zeros((groups, 2, 2, 2, groups, 2), np.float32)
    for d in range(groups):
        for a in range(2):
            for c in range(2):
                table[d, a, c, a, d, c] = 1
    return table.reshape(4 * groups, 4 * groups)


def dot(left, right):
    return lax.dot_general(left, right, (((1,), (0,)), ((), ())), preferred_element_type=f32)


def dot_nt(left, right):
    return lax.dot_general(left, right, (((1,), (1,)), ((), ())), preferred_element_type=f32)


def split(value):
    high = value.astype(bf16)
    low = (value - high.astype(f32)).astype(bf16)
    return high, low


def dot3(value, table_ref):
    high, low = split(value)
    top, bottom = table_ref[0], table_ref[1]
    return dot(high, top) + (dot(low, top) + dot(high, bottom))


def far_first(size):
    return sorted(range(size), key=lambda o: -min(o, size - o))


def exchange(groups, blocks, sig_hbm, cot_hbm, fil_hbm, *refs):
    tables_hbm, rest = refs[:7], refs[7:]
    out_gs, out_gf = rest[:2]
    sig, cot, fil = rest[2:5]
    both, filt, twist, forw, inv, back, perm = rest[5:12]
    (send, send_f, recv, recv_f, ready, ready_f) = rest[12:18]
    (load_sem, send_sem, recv_sem, send_f_sem, recv_f_sem) = rest[18:23]
    (gs_out_sem, gs_in_sem, gf_out_sem, gf_in_sem) = rest[23:]
    t = lax.axis_index("tp")
    p = lax.axis_index("cp")
    me = t * blocks + p
    devices = groups * blocks
    xs, lows = groups // 2, blocks // 8
    x, high = t // 2, lax.rem(t, 2)
    z, rest_p = high * lows + p // 8, lax.rem(p, 8)

    def greet_all():
        barrier = pltpu.get_barrier_semaphore()
        for z_off in far_first(2 * lows):
            z_to = lax.rem(z + z_off, 2 * lows)
            for x_off in far_first(xs):
                group = lax.rem(x + x_off, xs) * 2 + z_to // lows
                base = lax.rem(z_to, lows) * 8

                def greet(i, _, group=group, base=base):
                    place = base + lax.rem(rest_p + i, 8)
                    pl.semaphore_signal(
                        barrier, inc=1, device_id=(group, place), device_id_type=MESH
                    )
                    return 0

                lax.fori_loop(1 if z_off == 0 and x_off == 0 else 0, 8, greet, 0)

    steps = [(x_off, h_off) for x_off in far_first(xs) for h_off in (1, 0)]
    steps = sorted(steps, key=lambda o: min(o[0], xs - o[0]) + 0.5 * o[1])

    def there(step):
        return lax.rem(x + step[0], xs) * 2 + lax.rem(high + step[1], 2)

    def origin(step):
        return lax.rem(x + xs - step[0], xs) * 2 + lax.rem(high + step[1], 2)

    def places(step, act):
        def one(i, _):
            act(lax.rem(p + i, blocks))
            return 0

        lax.fori_loop(1 if step == (0, 0) else 0, blocks, one, 0)

    loads = [
        pltpu.make_async_copy(source, target, load_sem.at[i])
        for i, (source, target) in enumerate(
            zip(
                (sig_hbm, cot_hbm, fil_hbm) + tuple(tables_hbm),
                (sig, cot, fil, both, filt, twist, forw, inv, back, perm),
                strict=True,
            )
        )
    ]
    for load in loads:
        load.start()
    greet_all()
    for load in loads:
        load.wait()

    eye = identity()
    per = LANES // 2
    for q in range(2 * devices // LANES):
        cols = pl.ds(q * LANES, LANES)
        pair = jnp.concatenate([sig[:, cols], cot[:, cols]], axis=1)
        moved = dot_nt(perm[...], pair)
        send[pl.ds(q * per, per)] = moved.reshape(per, 4, LANES).astype(bf16)
        moved = dot_nt(eye, fil[:, cols])
        send_f[pl.ds(q * per, per)] = moved.reshape(per, 2, LANES).astype(bf16)

    pl.semaphore_wait(pltpu.get_barrier_semaphore(), devices - 1)

    pltpu.make_async_copy(send_f.at[me], recv_f.at[p], recv_f_sem).start()

    def give_filter(place):
        pltpu.make_async_remote_copy(
            send_f.at[t * blocks + place],
            recv_f.at[p],
            send_f_sem,
            recv_f_sem,
            device_id=(t, place),
            device_id_type=MESH,
        ).start()

    places((0, 0), give_filter)
    for n, step in enumerate(steps):
        group = there(step)

        def give(place, n=n, group=group):
            pltpu.make_async_remote_copy(
                send.at[group * blocks + place],
                recv.at[me],
                send_sem,
                recv_sem.at[n],
                device_id=(group, place),
                device_id_type=MESH,
            ).start()

        places(step, give)
        if step == (0, 0):
            pltpu.make_async_copy(send.at[me], recv.at[me], recv_sem.at[n]).start()

    turn_c, turn_s = twist[0], twist[1]
    width = 2 * blocks

    def spectrum(real, imag):
        turned = jnp.concatenate(
            [real * turn_c + imag * turn_s, imag * turn_c - real * turn_s], axis=1
        )
        return dot3(turned, forw)

    def inverse(real, imag):
        part = dot3(jnp.concatenate([real, imag], axis=1), inv)
        g_real, g_imag = part[:, :LANES], part[:, LANES:]
        turned = jnp.concatenate(
            [g_real * turn_c - g_imag * turn_s, g_real * turn_s + g_imag * turn_c], axis=0
        )
        high_part, low_part = split(turned)
        result = dot(back[...], jnp.concatenate([high_part, low_part, high_part], axis=0))
        return result.reshape(blocks, 2, LANES).astype(bf16)

    pltpu.make_async_copy(recv_f, recv_f, recv_f_sem).wait()
    data = recv_f[...].reshape(2 * blocks, LANES)
    halves = dot(filt[...], jnp.concatenate([data, data], axis=0))
    h_spec = spectrum(halves[:width], halves[width:])
    h_real, h_imag = h_spec[:, :LANES], h_spec[:, LANES:]

    sum_real = jnp.zeros((width, LANES), f32)
    sum_imag = jnp.zeros((width, LANES), f32)
    for n, step in enumerate(steps):
        group = origin(step)
        mine = pl.ds(group * blocks, blocks)
        pltpu.make_async_copy(recv.at[mine], recv.at[mine], recv_sem.at[n]).wait()
        data = recv[mine].reshape(4 * blocks, LANES)
        halves = dot(both[...], jnp.concatenate([data, data], axis=0))
        real = jnp.concatenate([halves[:width], halves[2 * width : 3 * width]], axis=0)
        imag = jnp.concatenate([halves[width : 2 * width], halves[3 * width :]], axis=0)
        cos2 = jnp.concatenate([turn_c, turn_c], axis=0)
        sin2 = jnp.concatenate([turn_s, turn_s], axis=0)
        turned = jnp.concatenate(
            [real * cos2 + imag * sin2, imag * cos2 - real * sin2], axis=1
        )
        spec = dot3(turned, forw)
        u_real, u_imag = spec[:width, :LANES], spec[:width, LANES:]
        d_real, d_imag = spec[width:, :LANES], spec[width:, LANES:]
        sum_real = sum_real + (u_real * d_real + u_imag * d_imag)
        sum_imag = sum_imag + (u_real * d_imag - u_imag * d_real)
        if n == len(steps) - 1:
            ready_f[...] = inverse(sum_real, sum_imag)
            for last in steps[::-1]:
                target = origin(last)

                def give_last(place, target=target):
                    pltpu.make_async_remote_copy(
                        ready_f.at[place],
                        out_gf.at[me],
                        gf_out_sem,
                        gf_in_sem,
                        device_id=(target, place),
                        device_id_type=MESH,
                    ).start()

                places(last, give_last)
            pltpu.make_async_copy(ready_f.at[p], out_gf.at[me], gf_in_sem).start()
        ready[mine] = inverse(
            h_real * d_real + h_imag * d_imag, h_real * d_imag - h_imag * d_real
        )

        def give_back(place, group=group):
            pltpu.make_async_remote_copy(
                ready.at[group * blocks + place],
                out_gs.at[me],
                gs_out_sem,
                gs_in_sem,
                device_id=(group, place),
                device_id_type=MESH,
            ).start()

        places(step, give_back)
        if step == (0, 0):
            pltpu.make_async_copy(ready.at[me], out_gs.at[me], gs_in_sem).start()

    some = pl.ds(0, devices - 1)
    pltpu.make_async_copy(send.at[some], send.at[some], send_sem).wait()
    pltpu.make_async_copy(ready.at[some], ready.at[some], gs_out_sem).wait()
    few = pl.ds(0, blocks - 1)
    pltpu.make_async_copy(send_f.at[few], send_f.at[few], send_f_sem).wait()
    pltpu.make_async_copy(out_gf.at[some], out_gf.at[some], gf_out_sem).wait()
    pltpu.make_async_copy(out_gs, out_gs, gs_in_sem).wait()
    pltpu.make_async_copy(out_gf, out_gf, gf_in_sem).wait()


def identity():
    rows = lax.broadcasted_iota(jnp.int32, (LANES, LANES), 0)
    cols = lax.broadcasted_iota(jnp.int32, (LANES, LANES), 1)
    return (rows == cols).astype(f32).astype(bf16)


def place_columns(quarters, gs_in, gf_in, gs_ref, gf_ref):
    eye = identity()
    per = LANES // 2
    for q in range(quarters):
        for source, target in ((gs_in, gs_ref), (gf_in, gf_ref)):
            block = source[pl.ds(q * per, per)].reshape(LANES, LANES)
            target[:, pl.ds(q * LANES, LANES)] = dot_nt(eye, block).astype(bf16)


def body(groups, blocks, signal, cotangent, long_filter):
    positions, columns = signal.shape
    devices = groups * blocks
    tables = make_tables(blocks) + (permutation(LANES // 2).astype(ml_dtypes.bfloat16),)
    vmem = pltpu.VMEM
    dma = pltpu.SemaphoreType.DMA
    anywhere = pl.BlockSpec(memory_space=pl.ANY)
    whole = pl.BlockSpec(memory_space=pltpu.VMEM)
    pairs = pltpu.VMEM((devices, 2, LANES), bf16)
    gs_rows, gf_rows = pl.pallas_call(
        functools.partial(exchange, groups, blocks),
        name="exchange",
        out_shape=(pairs, pairs),
        in_specs=[anywhere] * (3 + len(tables)),
        out_specs=(whole, whole),
        scratch_shapes=[vmem((positions, columns), bf16)] * 3
        + [vmem(table.shape, table.dtype) for table in tables]
        + [
            vmem((devices, 4, LANES), bf16),
            vmem((devices, 2, LANES), bf16),
            vmem((devices, 4, LANES), bf16),
            vmem((blocks, 2, LANES), bf16),
            vmem((devices, 2, LANES), bf16),
            vmem((blocks, 2, LANES), bf16),
            dma((3 + len(tables),)),
            dma(()),
            dma((groups,)),
            dma(()),
            dma(()),
            dma(()),
            dma(()),
            dma(()),
            dma(()),
        ],
        compiler_params=pltpu.CompilerParams(collective_id=0, has_side_effects=True),
    )(signal, cotangent, long_filter, *[jnp.asarray(table) for table in tables])
    gs_rows, gf_rows = (
        pltpu.with_memory_space_constraint(rows, pltpu.VMEM) for rows in (gs_rows, gf_rows)
    )
    result = jax.ShapeDtypeStruct((positions, columns), bf16)
    return pl.pallas_call(
        functools.partial(place_columns, columns // LANES),
        name="place_columns",
        out_shape=(result, result),
        in_specs=[whole] * 2,
        out_specs=(whole, whole),
    )(gs_rows, gf_rows)


def solution(mesh):
    in_specs = (P("cp", "tp"), P("cp", "tp"), P("cp", None))
    out_specs = (P("cp", "tp"), P("cp", None))
    run = functools.partial(body, mesh.shape["tp"], mesh.shape["cp"])
    return jax.shard_map(run, mesh=mesh, in_specs=in_specs, out_specs=out_specs, check_vma=False)
```

time: 47.5 us -> 41.4 us (0.87)
  Pallas kernels: 46.8 us -> 40.7 us
    pallas_call x1, Pallas kernels: 44.1 us -> 39.7 us  [body(): pl.pallas_call(functools.partial(exchange, groups, blocks), name='exchang...]
    pallas_call x1, Pallas kernels: 2.7 us -> 1 us  [body(): pl.pallas_call(functools.partial(place_columns, columns // LANES), name='...]
where the time goes in v1:
time: 41.4 us; the launch traced here: 41.3 us
  Pallas kernels  40.7 us (98%)
  between operations  0.64 us (2%)
    pallas_call x1, Pallas kernels, body(): pl.pallas_call(functools.partial(exchange, groups, blocks), name='exchang...  39.7 us
    pallas_call x1, Pallas kernels, body(): pl.pallas_call(functools.partial(place_columns, columns // LANES), name='...  1 us

profile of v1, /device:TPU:1, one launch (start us, length us, event | category | flops | bytes accessed | tf_op | source)
XLA Modules:
  0.0 41.3 jit_solution(7293248371127714275)
XLA Ops:
  0.6 39.7 %exchange.1 = (bf16[256,2,128]{2,1,0:T(2,128)(2,1)S(1)}, bf16[256,2,128]{2,1,0:T(2,128)(2,1)S(1)}) custom-call(bf16[128,512]{1,0:T(8,128)(2,1)} %sig_hbm.1, bf16[128,512]{1,0:T(8,128)(2,1)} %cot_hbm.1, bf16[128,512]{1,0:T(8,128)(2,1)} %fil_hbm.1, bf16[256,256]{1,0:T(8,128)(2,1)} %constant.14.clone.refs_0_, bf16[128,128]{1,0:T(8,128)(2,1)} %constant.15.clone.refs_1_, ...), custom_call_target="tpu_custom_call" | custom-call | tf_op jit(solution)/shard_map/exchange/pallas_call | solution.py:314
  40.3 1.0 %place_columns.1 = (bf16[128,512]{1,0:T(8,128)(2,1)}, bf16[128,512]{1,0:T(8,128)(2,1)}) custom-call(bf16[256,2,128]{2,1,0:T(2,128)(2,1)S(1)} %get-tuple-element.4.gs_in, bf16[256,2,128]{2,1,0:T(2,128)(2,1)S(1)} %get-tuple-element.5.gf_in), custom_call_target="tpu_custom_call" | custom-call | tf_op jit(solution)/shard_map/place_columns/pallas_call | solution.py:345

commit v2 on v1

--- a/solution.py
+++ b/solution.py
@@ -121,10 +121,13 @@
                     )
                     return 0
 
-                lax.fori_loop(1 if z_off == 0 and x_off == 0 else 0, 8, greet, 0)
+                lax.fori_loop(
+                    1 if z_off == 0 and x_off == 0 else 0, 8, greet, 0, unroll=True
+                )
 
     steps = [(x_off, h_off) for x_off in far_first(xs) for h_off in (1, 0)]
-    steps = sorted(steps, key=lambda o: min(o[0], xs - o[0]) + 0.5 * o[1])
+    steps = sorted(steps, key=lambda o: -min(o[0], xs - o[0]) - 0.5 * o[1])
+    sizes = (groups // 2, groups // 2)
 
     def there(step):
         return lax.rem(x + step[0], xs) * 2 + lax.rem(high + step[1], 2)
@@ -137,7 +140,7 @@
             act(lax.rem(p + i, blocks))
             return 0
 
-        lax.fori_loop(1 if step == (0, 0) else 0, blocks, one, 0)
+        lax.fori_loop(1 if step == (0, 0) else 0, blocks, one, 0, unroll=8)
 
     loads = [
         pltpu.make_async_copy(source, target, load_sem.at[i])
@@ -179,8 +182,9 @@
             device_id_type=MESH,
         ).start()
 
-    places((0, 0), give_filter)
     for n, step in enumerate(steps):
+        if n == len(steps) // 2:
+            places((0, 0), give_filter)
         group = there(step)
 
         def give(place, n=n, group=group):
@@ -194,76 +198,42 @@
             ).start()
 
         places(step, give)
-        if step == (0, 0):
+        if tuple(step) == (0, 0):
             pltpu.make_async_copy(send.at[me], recv.at[me], recv_sem.at[n]).start()
 
     turn_c, turn_s = twist[0], twist[1]
     width = 2 * blocks
 
-    def spectrum(real, imag):
-        turned = jnp.concatenate(
+    def turn(real, imag):
+        return jnp.concatenate(
             [real * turn_c + imag * turn_s, imag * turn_c - real * turn_s], axis=1
         )
-        return dot3(turned, forw)
-
-    def inverse(real, imag):
-        part = dot3(jnp.concatenate([real, imag], axis=1), inv)
+
+    def unturn(part):
         g_real, g_imag = part[:, :LANES], part[:, LANES:]
-        turned = jnp.concatenate(
+        return jnp.concatenate(
             [g_real * turn_c - g_imag * turn_s, g_real * turn_s + g_imag * turn_c], axis=0
         )
-        high_part, low_part = split(turned)
-        result = dot(back[...], jnp.concatenate([high_part, low_part, high_part], axis=0))
-        return result.reshape(blocks, 2, LANES).astype(bf16)
-
-    pltpu.make_async_copy(recv_f, recv_f, recv_f_sem).wait()
-    data = recv_f[...].reshape(2 * blocks, LANES)
-    halves = dot(filt[...], jnp.concatenate([data, data], axis=0))
-    h_spec = spectrum(halves[:width], halves[width:])
-    h_real, h_imag = h_spec[:, :LANES], h_spec[:, LANES:]
-
-    sum_real = jnp.zeros((width, LANES), f32)
-    sum_imag = jnp.zeros((width, LANES), f32)
-    for n, step in enumerate(steps):
+
+    def inverse(spectra):
+        part = dot3(
+            jnp.concatenate([jnp.concatenate(pair, axis=1) for pair in spectra], axis=0), inv
+        )
+        turned = [unturn(part[i * width : (i + 1) * width]) for i in range(len(spectra))]
+        results = []
+        for i in range(0, len(turned), 2):
+            some = turned[i : i + 2]
+            high_part, low_part = split(jnp.concatenate(some, axis=1))
+            rows = dot(back[...], jnp.concatenate([high_part, low_part, high_part], axis=0))
+            for n in range(len(some)):
+                result = rows[:, n * LANES : (n + 1) * LANES]
+                results.append(result.reshape(blocks, 2, LANES).astype(bf16))
+        return results
+
+    def give_rows(step):
         group = origin(step)
-        mine = pl.ds(group * blocks, blocks)
-        pltpu.make_async_copy(recv.at[mine], recv.at[mine], recv_sem.at[n]).wait()
-        data = recv[mine].reshape(4 * blocks, LANES)
-        halves = dot(both[...], jnp.concatenate([data, data], axis=0))
-        real = jnp.concatenate([halves[:width], halves[2 * width : 3 * width]], axis=0)
-        imag = jnp.concatenate([halves[width : 2 * width], halves[3 * width :]], axis=0)
-        cos2 = jnp.concatenate([turn_c, turn_c], axis=0)
-        sin2 = jnp.concatenate([turn_s, turn_s], axis=0)
-        turned = jnp.concatenate(
-            [real * cos2 + imag * sin2, imag * cos2 - real * sin2], axis=1
-        )
-        spec = dot3(turned, forw)
-        u_real, u_imag = spec[:width, :LANES], spec[:width, LANES:]
-        d_real, d_imag = spec[width:, :LANES], spec[width:, LANES:]
-        sum_real = sum_real + (u_real * d_real + u_imag * d_imag)
-        sum_imag = sum_imag + (u_real * d_imag - u_imag * d_real)
-        if n == len(steps) - 1:
-            ready_f[...] = inverse(sum_real, sum_imag)
-            for last in steps[::-1]:
-                target = origin(last)
-
-                def give_last(place, target=target):
-                    pltpu.make_async_remote_copy(
-                        ready_f.at[place],
-                        out_gf.at[me],
-                        gf_out_sem,
-                        gf_in_sem,
-                        device_id=(target, place),
-                        device_id_type=MESH,
-                    ).start()
-
-                places(last, give_last)
-            pltpu.make_async_copy(ready_f.at[p], out_gf.at[me], gf_in_sem).start()
-        ready[mine] = inverse(
-            h_real * d_real + h_imag * d_imag, h_real * d_imag - h_imag * d_real
-        )
-
-        def give_back(place, group=group):
+
+        def give_back(place):
             pltpu.make_async_remote_copy(
                 ready.at[group * blocks + place],
                 out_gs.at[me],
@@ -276,6 +246,72 @@
         places(step, give_back)
         if step == (0, 0):
             pltpu.make_async_copy(ready.at[me], out_gs.at[me], gs_in_sem).start()
+
+    def give_sums(step):
+        group = origin(step)
+
+        def give_last(place):
+            pltpu.make_async_remote_copy(
+                ready_f.at[place],
+                out_gf.at[me],
+                gf_out_sem,
+                gf_in_sem,
+                device_id=(group, place),
+                device_id_type=MESH,
+            ).start()
+
+        places(step, give_last)
+        if step == (0, 0):
+            pltpu.make_async_copy(ready_f.at[p], out_gf.at[me], gf_in_sem).start()
+
+    pltpu.make_async_copy(recv_f, recv_f, recv_f_sem).wait()
+    data = recv_f[...].reshape(2 * blocks, LANES)
+    halves = dot(filt[...], jnp.concatenate([data, data], axis=0))
+    h_spec = dot3(turn(halves[:width], halves[width:]), forw)
+    h_real, h_imag = h_spec[:, :LANES], h_spec[:, LANES:]
+
+    sum_real = jnp.zeros((width, LANES), f32)
+    sum_imag = jnp.zeros((width, LANES), f32)
+    first = 0
+    for size in sizes:
+        some = range(first, first + size)
+        first += size
+        mine = [pl.ds(origin(steps[n]) * blocks, blocks) for n in some]
+        for n, rows in zip(some, mine, strict=True):
+            pltpu.make_async_copy(recv.at[rows], recv.at[rows], recv_sem.at[n]).wait()
+        turned = []
+        for i in range(0, size, 2):
+            data = jnp.concatenate(
+                [recv[rows].reshape(4 * blocks, LANES) for rows in mine[i : i + 2]], axis=1
+            )
+            halves = dot(both[...], jnp.concatenate([data, data], axis=0))
+            for n in range(len(mine[i : i + 2])):
+                part = halves[:, n * LANES : (n + 1) * LANES]
+                turned.append(turn(part[:width], part[width : 2 * width]))
+                turned.append(turn(part[2 * width : 3 * width], part[3 * width :]))
+        spec = dot3(jnp.concatenate(turned, axis=0), forw)
+        products = []
+        for n in range(size):
+            u_spec = spec[2 * n * width : (2 * n + 1) * width]
+            d_spec = spec[(2 * n + 1) * width : (2 * n + 2) * width]
+            u_real, u_imag = u_spec[:, :LANES], u_spec[:, LANES:]
+            d_real, d_imag = d_spec[:, :LANES], d_spec[:, LANES:]
+            sum_real = sum_real + (u_real * d_real + u_imag * d_imag)
+            sum_imag = sum_imag + (u_real * d_imag - u_imag * d_real)
+            products.append(
+                (h_real * d_real + h_imag * d_imag, h_real * d_imag - h_imag * d_real)
+            )
+        if first == len(steps):
+            products.append((sum_real, sum_imag))
+        results = inverse(products)
+        if first == len(steps):
+            ready_f[...] = results[-1]
+            for step in steps:
+                give_sums(step)
+        for rows, result in zip(mine, results[:size], strict=True):
+            ready[rows] = result
+        for n in some:
+            give_rows(steps[n])
 
     some = pl.ds(0, devices - 1)
     pltpu.make_async_copy(send.at[some], send.at[some], send_sem).wait()

time: 41.4 us -> 37.3 us (0.901)
  Pallas kernels: 40.7 us -> 36.6 us
    pallas_call x1, Pallas kernels: 39.7 us -> 35.6 us  [body(): pl.pallas_call(functools.partial(exchange, groups, blocks), name='exchang...]
where the time goes in v2:
time: 37.3 us; the launch traced here: 37.2 us
  Pallas kernels  36.6 us (98%)
  between operations  0.64 us (2%)
    pallas_call x1, Pallas kernels, body(): pl.pallas_call(functools.partial(exchange, groups, blocks), name='exchang...  35.6 us
    pallas_call x1, Pallas kernels, body(): pl.pallas_call(functools.partial(place_columns, columns // LANES), name='...  1 us

profile of v2, /device:TPU:1, one launch (start us, length us, event | category | flops | bytes accessed | tf_op | source)
XLA Modules:
  0.0 37.2 jit_solution(12327027980783642187)
XLA Ops:
  0.6 35.6 %exchange.1 = (bf16[256,2,128]{2,1,0:T(2,128)(2,1)S(1)}, bf16[256,2,128]{2,1,0:T(2,128)(2,1)S(1)}) custom-call(bf16[128,512]{1,0:T(8,128)(2,1)} %sig_hbm.1, bf16[128,512]{1,0:T(8,128)(2,1)} %cot_hbm.1, bf16[128,512]{1,0:T(8,128)(2,1)} %fil_hbm.1, bf16[256,256]{1,0:T(8,128)(2,1)} %constant.14.clone.refs_0_, bf16[128,128]{1,0:T(8,128)(2,1)} %constant.15.clone.refs_1_, ...), custom_call_target="tpu_custom_call" | custom-call | tf_op jit(solution)/shard_map/exchange/pallas_call | solution.py:350
  36.2 1.0 %place_columns.1 = (bf16[128,512]{1,0:T(8,128)(2,1)}, bf16[128,512]{1,0:T(8,128)(2,1)}) custom-call(bf16[256,2,128]{2,1,0:T(2,128)(2,1)S(1)} %get-tuple-element.4.gs_in, bf16[256,2,128]{2,1,0:T(2,128)(2,1)S(1)} %get-tuple-element.5.gf_in), custom_call_target="tpu_custom_call" | custom-call | tf_op jit(solution)/shard_map/place_columns/pallas_call | solution.py:381

commit v3 on v2

--- a/solution.py
+++ b/solution.py
@@ -127,7 +127,7 @@
 
     steps = [(x_off, h_off) for x_off in far_first(xs) for h_off in (1, 0)]
     steps = sorted(steps, key=lambda o: -min(o[0], xs - o[0]) - 0.5 * o[1])
-    sizes = (groups // 2, groups // 2)
+    sizes = (groups // 4, groups // 4, groups // 2)
 
     def there(step):
         return lax.rem(x + step[0], xs) * 2 + lax.rem(high + step[1], 2)
@@ -183,7 +183,7 @@
         ).start()
 
     for n, step in enumerate(steps):
-        if n == len(steps) // 2:
+        if n == len(steps) // 4:
             places((0, 0), give_filter)
         group = there(step)
 
@@ -247,22 +247,29 @@
         if step == (0, 0):
             pltpu.make_async_copy(ready.at[me], out_gs.at[me], gs_in_sem).start()
 
-    def give_sums(step):
-        group = origin(step)
-
-        def give_last(place):
-            pltpu.make_async_remote_copy(
-                ready_f.at[place],
-                out_gf.at[me],
-                gf_out_sem,
-                gf_in_sem,
-                device_id=(group, place),
-                device_id_type=MESH,
-            ).start()
-
-        places(step, give_last)
-        if step == (0, 0):
-            pltpu.make_async_copy(ready_f.at[p], out_gf.at[me], gf_in_sem).start()
+    def give_sums(half):
+        for x_off in far_first(xs):
+            group = lax.rem(x + xs - x_off, xs) * 2 + half
+
+            def give_last(i, _, group=group):
+                place = lax.rem(p + i, blocks)
+                pltpu.make_async_remote_copy(
+                    ready_f.at[place],
+                    out_gf.at[me],
+                    gf_out_sem,
+                    gf_in_sem,
+                    device_id=(group, place),
+                    device_id_type=MESH,
+                ).start()
+                return 0
+
+            if x_off == 0:
+                @pl.when(group != t)
+                def _():
+                    give_last(0, 0)
+            else:
+                give_last(0, 0)
+            lax.fori_loop(1, blocks, give_last, 0, unroll=8)
 
     pltpu.make_async_copy(recv_f, recv_f, recv_f_sem).wait()
     data = recv_f[...].reshape(2 * blocks, LANES)
@@ -306,12 +313,13 @@
         results = inverse(products)
         if first == len(steps):
             ready_f[...] = results[-1]
-            for step in steps:
-                give_sums(step)
+            pltpu.make_async_copy(ready_f.at[p], out_gf.at[me], gf_in_sem).start()
+            give_sums(0)
         for rows, result in zip(mine, results[:size], strict=True):
             ready[rows] = result
-        for n in some:
+        for n in sorted(some, key=lambda n: -steps[n][1]):
             give_rows(steps[n])
+    give_sums(1)
 
     some = pl.ds(0, devices - 1)
     pltpu.make_async_copy(send.at[some], send.at[some], send_sem).wait()

time: 37.3 us -> 35.8 us (0.960)
  Pallas kernels: 36.6 us -> 35.1 us
    pallas_call x1, Pallas kernels: 35.6 us -> 34.1 us  [body(): pl.pallas_call(functools.partial(exchange, groups, blocks), name='exchang...]
where the time goes in v3:
time: 35.8 us
  Pallas kernels  35.1 us (98%)
  between operations  0.64 us (2%)
    pallas_call x1, Pallas kernels, body(): pl.pallas_call(functools.partial(exchange, groups, blocks), name='exchang...  34.1 us
    pallas_call x1, Pallas kernels, body(): pl.pallas_call(functools.partial(place_columns, columns // LANES), name='...  1 us

profile of v3, /device:TPU:1, one launch (start us, length us, event | category | flops | bytes accessed | tf_op | source)
XLA Modules:
  0.0 35.8 jit_solution(12299143215264688421)
XLA Ops:
  0.6 34.1 %exchange.1 = (bf16[256,2,128]{2,1,0:T(2,128)(2,1)S(1)}, bf16[256,2,128]{2,1,0:T(2,128)(2,1)S(1)}) custom-call(bf16[128,512]{1,0:T(8,128)(2,1)} %sig_hbm.1, bf16[128,512]{1,0:T(8,128)(2,1)} %cot_hbm.1, bf16[128,512]{1,0:T(8,128)(2,1)} %fil_hbm.1, bf16[256,256]{1,0:T(8,128)(2,1)} %constant.14.clone.refs_0_, bf16[128,128]{1,0:T(8,128)(2,1)} %constant.15.clone.refs_1_, ...), custom_call_target="tpu_custom_call" | custom-call | tf_op jit(solution)/shard_map/exchange/pallas_call | solution.py:358
  34.8 1.0 %place_columns.1 = (bf16[128,512]{1,0:T(8,128)(2,1)}, bf16[128,512]{1,0:T(8,128)(2,1)}) custom-call(bf16[256,2,128]{2,1,0:T(2,128)(2,1)S(1)} %get-tuple-element.4.gs_in, bf16[256,2,128]{2,1,0:T(2,128)(2,1)S(1)} %get-tuple-element.5.gf_in), custom_call_target="tpu_custom_call" | custom-call | tf_op jit(solution)/shard_map/place_columns/pallas_call | solution.py:389

commit v4 on v3

--- a/solution.py
+++ b/solution.py
@@ -106,9 +106,12 @@
     x, high = t // 2, lax.rem(t, 2)
     z, rest_p = high * lows + p // 8, lax.rem(p, 8)
 
-    def greet_all():
+    def greet_all(loads):
         barrier = pltpu.get_barrier_semaphore()
         for z_off in far_first(2 * lows):
+            if z_off == lows - 2:
+                for load in loads:
+                    load.start()
             z_to = lax.rem(z + z_off, 2 * lows)
             for x_off in far_first(xs):
                 group = lax.rem(x + x_off, xs) * 2 + z_to // lows
@@ -152,9 +155,7 @@
             )
         )
     ]
-    for load in loads:
-        load.start()
-    greet_all()
+    greet_all(loads)
     for load in loads:
         load.wait()
 
@@ -230,46 +231,58 @@
                 results.append(result.reshape(blocks, 2, LANES).astype(bf16))
         return results
 
-    def give_rows(step):
+    head = 1
+    turn_to_head = lax.rem(head - p + blocks, blocks)
+
+    def all_but_head(group, act):
+        def one(i, _):
+            act(lax.rem(p + i, blocks))
+            return 0
+
+        @pl.when(jnp.logical_and(group != t, p != head))
+        def _():
+            act(p)
+
+        lax.fori_loop(1, turn_to_head, one, 0)
+        lax.fori_loop(turn_to_head + 1, blocks, one, 0)
+
+        @pl.when(jnp.logical_and(group != 0, jnp.logical_or(group != t, p != head)))
+        def _():
+            act(head)
+
+    def give_row(group, place):
+        pltpu.make_async_remote_copy(
+            ready.at[group * blocks + place],
+            out_gs.at[me],
+            gs_out_sem,
+            gs_in_sem,
+            device_id=(group, place),
+            device_id_type=MESH,
+        ).start()
+
+    def give_rows(step, late):
         group = origin(step)
-
-        def give_back(place):
-            pltpu.make_async_remote_copy(
-                ready.at[group * blocks + place],
-                out_gs.at[me],
-                gs_out_sem,
-                gs_in_sem,
-                device_id=(group, place),
-                device_id_type=MESH,
-            ).start()
-
-        places(step, give_back)
+        if late:
+            all_but_head(group, functools.partial(give_row, group))
+        else:
+            places(step, functools.partial(give_row, group))
         if step == (0, 0):
             pltpu.make_async_copy(ready.at[me], out_gs.at[me], gs_in_sem).start()
+
+    def give_sum(group, place):
+        pltpu.make_async_remote_copy(
+            ready_f.at[place],
+            out_gf.at[me],
+            gf_out_sem,
+            gf_in_sem,
+            device_id=(group, place),
+            device_id_type=MESH,
+        ).start()
 
     def give_sums(half):
         for x_off in far_first(xs):
             group = lax.rem(x + xs - x_off, xs) * 2 + half
-
-            def give_last(i, _, group=group):
-                place = lax.rem(p + i, blocks)
-                pltpu.make_async_remote_copy(
-                    ready_f.at[place],
-                    out_gf.at[me],
-                    gf_out_sem,
-                    gf_in_sem,
-                    device_id=(group, place),
-                    device_id_type=MESH,
-                ).start()
-                return 0
-
-            if x_off == 0:
-                @pl.when(group != t)
-                def _():
-                    give_last(0, 0)
-            else:
-                give_last(0, 0)
-            lax.fori_loop(1, blocks, give_last, 0, unroll=8)
+            all_but_head(group, functools.partial(give_sum, group))
 
     pltpu.make_async_copy(recv_f, recv_f, recv_f_sem).wait()
     data = recv_f[...].reshape(2 * blocks, LANES)
@@ -311,14 +324,27 @@
         if first == len(steps):
             products.append((sum_real, sum_imag))
         results = inverse(products)
-        if first == len(steps):
+        late = first == len(steps)
+        if late:
             ready_f[...] = results[-1]
-            pltpu.make_async_copy(ready_f.at[p], out_gf.at[me], gf_in_sem).start()
-            give_sums(0)
         for rows, result in zip(mine, results[:size], strict=True):
             ready[rows] = result
+        if late:
+            pltpu.make_async_copy(ready_f.at[p], out_gf.at[me], gf_in_sem).start()
+
+            @pl.when(me != head)
+            def _():
+                give_sum(0, head)
+
+            for n in some:
+
+                @pl.when(jnp.logical_and(origin(steps[n]) == 0, me != head))
+                def _():
+                    give_row(0, head)
+
+            give_sums(0)
         for n in sorted(some, key=lambda n: -steps[n][1]):
-            give_rows(steps[n])
+            give_rows(steps[n], late)
     give_sums(1)
 
     some = pl.ds(0, devices - 1)

time: 35.8 us -> 34.8 us (0.972); the launches traced: 35.8 us -> 34.2 us
  Pallas kernels: 35.1 us -> 33.6 us
    pallas_call x1, Pallas kernels: 34.1 us -> 32.5 us  [body(): pl.pallas_call(functools.partial(exchange, groups, blocks), name='exchang...]
where the time goes in v4:
time: 34.8 us; the launch traced here: 34.2 us
  Pallas kernels  33.6 us (97%)
  between operations  0.64 us (2%)
    pallas_call x1, Pallas kernels, body(): pl.pallas_call(functools.partial(exchange, groups, blocks), name='exchang...  32.5 us
    pallas_call x1, Pallas kernels, body(): pl.pallas_call(functools.partial(place_columns, columns // LANES), name='...  1 us

profile of v4, /device:TPU:1, one launch (start us, length us, event | category | flops | bytes accessed | tf_op | source)
XLA Modules:
  0.0 34.2 jit_solution(4647365641411657344)
XLA Ops:
  0.6 32.5 %exchange.1 = (bf16[256,2,128]{2,1,0:T(2,128)(2,1)S(1)}, bf16[256,2,128]{2,1,0:T(2,128)(2,1)S(1)}) custom-call(bf16[128,512]{1,0:T(8,128)(2,1)} %sig_hbm.1, bf16[128,512]{1,0:T(8,128)(2,1)} %cot_hbm.1, bf16[128,512]{1,0:T(8,128)(2,1)} %fil_hbm.1, bf16[256,256]{1,0:T(8,128)(2,1)} %constant.14.clone.refs_0_, bf16[128,128]{1,0:T(8,128)(2,1)} %constant.15.clone.refs_1_, ...), custom_call_target="tpu_custom_call" | custom-call | tf_op jit(solution)/shard_map/exchange/pallas_call | solution.py:384
  33.2 1.0 %place_columns.1 = (bf16[128,512]{1,0:T(8,128)(2,1)}, bf16[128,512]{1,0:T(8,128)(2,1)}) custom-call(bf16[256,2,128]{2,1,0:T(2,128)(2,1)S(1)} %get-tuple-element.4.gs_in, bf16[256,2,128]{2,1,0:T(2,128)(2,1)S(1)} %get-tuple-element.5.gf_in), custom_call_target="tpu_custom_call" | custom-call | tf_op jit(solution)/shard_map/place_columns/pallas_call | solution.py:415

commit v5 on v4

--- a/solution.py
+++ b/solution.py
@@ -239,16 +239,22 @@
             act(lax.rem(p + i, blocks))
             return 0
 
-        @pl.when(jnp.logical_and(group != t, p != head))
+        @pl.when(group == 0)
         def _():
-            act(p)
-
-        lax.fori_loop(1, turn_to_head, one, 0)
-        lax.fori_loop(turn_to_head + 1, blocks, one, 0)
-
-        @pl.when(jnp.logical_and(group != 0, jnp.logical_or(group != t, p != head)))
+            @pl.when(jnp.logical_and(t != 0, p != head))
+            def _():
+                act(p)
+
+            lax.fori_loop(1, turn_to_head, one, 0)
+            lax.fori_loop(turn_to_head + 1, blocks, one, 0)
+
+        @pl.when(group != 0)
         def _():
-            act(head)
+            @pl.when(group != t)
+            def _():
+                act(p)
+
+            lax.fori_loop(1, blocks, one, 0, unroll=8)
 
     def give_row(group, place):
         pltpu.make_async_remote_copy(

time: 34.8 us -> 34.3 us (0.986); the launches traced: 34.2 us -> 34.2 us
  no operation moved by 1% of the time
where the time goes in v5:
time: 34.3 us; the launch traced here: 34.2 us
  Pallas kernels  33.6 us (98%)
  between operations  0.64 us (2%)
    pallas_call x1, Pallas kernels, body(): pl.pallas_call(functools.partial(exchange, groups, blocks), name='exchang...  32.6 us
    pallas_call x1, Pallas kernels, body(): pl.pallas_call(functools.partial(place_columns, columns // LANES), name='...  1 us

profile of v5, /device:TPU:1, one launch (start us, length us, event | category | flops | bytes accessed | tf_op | source)
XLA Modules:
  0.0 34.2 jit_solution(13664369068290964673)
XLA Ops:
  0.6 32.6 %exchange.1 = (bf16[256,2,128]{2,1,0:T(2,128)(2,1)S(1)}, bf16[256,2,128]{2,1,0:T(2,128)(2,1)S(1)}) custom-call(bf16[128,512]{1,0:T(8,128)(2,1)} %sig_hbm.1, bf16[128,512]{1,0:T(8,128)(2,1)} %cot_hbm.1, bf16[128,512]{1,0:T(8,128)(2,1)} %fil_hbm.1, bf16[256,256]{1,0:T(8,128)(2,1)} %constant.14.clone.refs_0_, bf16[128,128]{1,0:T(8,128)(2,1)} %constant.15.clone.refs_1_, ...), custom_call_target="tpu_custom_call" | custom-call | tf_op jit(solution)/shard_map/exchange/pallas_call | solution.py:390
  33.2 1.0 %place_columns.1 = (bf16[128,512]{1,0:T(8,128)(2,1)}, bf16[128,512]{1,0:T(8,128)(2,1)}) custom-call(bf16[256,2,128]{2,1,0:T(2,128)(2,1)S(1)} %get-tuple-element.4.gs_in, bf16[256,2,128]{2,1,0:T(2,128)(2,1)S(1)} %get-tuple-element.5.gf_in), custom_call_target="tpu_custom_call" | custom-call | tf_op jit(solution)/shard_map/place_columns/pallas_call | solution.py:421

commit v6 on v5

--- a/solution.py
+++ b/solution.py
@@ -109,7 +109,7 @@
     def greet_all(loads):
         barrier = pltpu.get_barrier_semaphore()
         for z_off in far_first(2 * lows):
-            if z_off == lows - 2:
+            if z_off == 0:
                 for load in loads:
                     load.start()
             z_to = lax.rem(z + z_off, 2 * lows)

time: 34.3 us -> 34.3 us (level)
  no operation moved by 1% of the time
where the time goes in v6:
time: 34.3 us; the launch traced here: 34.2 us
  Pallas kernels  33.6 us (98%)
  between operations  0.64 us (2%)
    pallas_call x1, Pallas kernels, body(): pl.pallas_call(functools.partial(exchange, groups, blocks), name='exchang...  32.6 us
    pallas_call x1, Pallas kernels, body(): pl.pallas_call(functools.partial(place_columns, columns // LANES), name='...  1 us

profile of v6, /device:TPU:1, one launch (start us, length us, event | category | flops | bytes accessed | tf_op | source)
XLA Modules:
  0.0 34.2 jit_solution(9143497745116098520)
XLA Ops:
  0.6 32.6 %exchange.1 = (bf16[256,2,128]{2,1,0:T(2,128)(2,1)S(1)}, bf16[256,2,128]{2,1,0:T(2,128)(2,1)S(1)}) custom-call(bf16[128,512]{1,0:T(8,128)(2,1)} %sig_hbm.1, bf16[128,512]{1,0:T(8,128)(2,1)} %cot_hbm.1, bf16[128,512]{1,0:T(8,128)(2,1)} %fil_hbm.1, bf16[256,256]{1,0:T(8,128)(2,1)} %constant.14.clone.refs_0_, bf16[128,128]{1,0:T(8,128)(2,1)} %constant.15.clone.refs_1_, ...), custom_call_target="tpu_custom_call" | custom-call | tf_op jit(solution)/shard_map/exchange/pallas_call | solution.py:390
  33.2 1.0 %place_columns.1 = (bf16[128,512]{1,0:T(8,128)(2,1)}, bf16[128,512]{1,0:T(8,128)(2,1)}) custom-call(bf16[256,2,128]{2,1,0:T(2,128)(2,1)S(1)} %get-tuple-element.4.gs_in, bf16[256,2,128]{2,1,0:T(2,128)(2,1)S(1)} %get-tuple-element.5.gf_in), custom_call_target="tpu_custom_call" | custom-call | tf_op jit(solution)/shard_map/place_columns/pallas_call | solution.py:421

commit v7 on v6

--- a/solution.py
+++ b/solution.py
@@ -184,7 +184,7 @@
         ).start()
 
     for n, step in enumerate(steps):
-        if n == len(steps) // 4:
+        if n == 1:
             places((0, 0), give_filter)
         group = there(step)
 

time: 34.3 us -> 34.3 us (level)
  no operation moved by 1% of the time
where the time goes in v7:
time: 34.3 us; the launch traced here: 34.2 us
  Pallas kernels  33.6 us (98%)
  between operations  0.64 us (2%)
    pallas_call x1, Pallas kernels, body(): pl.pallas_call(functools.partial(exchange, groups, blocks), name='exchang...  32.6 us
    pallas_call x1, Pallas kernels, body(): pl.pallas_call(functools.partial(place_columns, columns // LANES), name='...  1 us

profile of v7, /device:TPU:1, one launch (start us, length us, event | category | flops | bytes accessed | tf_op | source)
XLA Modules:
  0.0 34.2 jit_solution(8621248490038469333)
XLA Ops:
  0.6 32.6 %exchange.1 = (bf16[256,2,128]{2,1,0:T(2,128)(2,1)S(1)}, bf16[256,2,128]{2,1,0:T(2,128)(2,1)S(1)}) custom-call(bf16[128,512]{1,0:T(8,128)(2,1)} %sig_hbm.1, bf16[128,512]{1,0:T(8,128)(2,1)} %cot_hbm.1, bf16[128,512]{1,0:T(8,128)(2,1)} %fil_hbm.1, bf16[256,256]{1,0:T(8,128)(2,1)} %constant.14.clone.refs_0_, bf16[128,128]{1,0:T(8,128)(2,1)} %constant.15.clone.refs_1_, ...), custom_call_target="tpu_custom_call" | custom-call | tf_op jit(solution)/shard_map/exchange/pallas_call | solution.py:390
  33.2 1.0 %place_columns.1 = (bf16[128,512]{1,0:T(8,128)(2,1)}, bf16[128,512]{1,0:T(8,128)(2,1)}) custom-call(bf16[256,2,128]{2,1,0:T(2,128)(2,1)S(1)} %get-tuple-element.4.gs_in, bf16[256,2,128]{2,1,0:T(2,128)(2,1)S(1)} %get-tuple-element.5.gf_in), custom_call_target="tpu_custom_call" | custom-call | tf_op jit(solution)/shard_map/place_columns/pallas_call | solution.py:421
